TPU v7x, 512 devices: a whole 4x4x16 slice. The times are simulated.
512 devices in a mesh: dp: 8 (over x_hi, y), fsdp: 16 (over z), tensor: 4 (over x_lo, core).
Axes of the slice: x: 4 (x_hi: 2, x_lo: 2; x = x_hi * 2 + x_lo), y: 4, z: 16, core: 2. Of those that a mesh axis runs over, the one named last changes fastest.
Arguments:
- grad_part: bfloat16 [8, 16, 2048, 1024], P('dp', 'fsdp', None, 'tensor'), may hold values from -900 to 900
- gain_grad_part: bfloat16 [8, 16, 4, 2048], P('dp', 'fsdp', 'tensor'), may hold values from -840 to 840
- master: float32 [2048, 1024], P('fsdp', 'tensor'), may hold values from -0.005 to 0.005
- moment_one: float32 [2048, 1024], P('fsdp', 'tensor'), may hold values from -2.4 to 2.4
- moment_two: float32 [2048, 1024], P('fsdp', 'tensor'), may hold values from 0.05 to 1.5
- teacher: float32 [2048, 1024], P('fsdp', 'tensor'), may hold values from -0.005 to 0.005
- gain_master: float32 [2048], P('fsdp'), may hold values from -0.008 to 0.008
- gain_moment_one: float32 [2048], P('fsdp'), may hold values from -18 to 18
- gain_moment_two: float32 [2048], P('fsdp'), may hold values from 2 to 32
- gain_teacher: float32 [2048], P('fsdp'), may hold values from -0.008 to 0.008
Outputs:
- weights: bfloat16 [2048, 1024], P(None, 'tensor')
- gain_weights: bfloat16 [2048], replicated
- master_new: float32 [2048, 1024], P('fsdp', 'tensor')
- moment_one_new: float32 [2048, 1024], P('fsdp', 'tensor')
- moment_two_new: float32 [2048, 1024], P('fsdp', 'tensor')
- teacher_new: float32 [2048, 1024], P('fsdp', 'tensor')
- gain_master_new: float32 [2048], P('fsdp')
- gain_moment_one_new: float32 [2048], P('fsdp')
- gain_moment_two_new: float32 [2048], P('fsdp')
- gain_teacher_new: float32 [2048], P('fsdp')
All inputs are finite; a program needn't handle non-finite values.
Results may differ from a plain program's by a relative error of at most 0.001.
Values may be sent and summed in bfloat16 or wider, within the bound.
No kernel may reach another device: no remote copies, remote signals or barrier semaphores. Data moves between devices by JAX's collectives and lax.ppermute only.
A program may use at most 64 MiB of HBM per device.

v0:
```python
import math
import jax
import jax.numpy as jnp
from jax import lax
from jax.sharding import PartitionSpec as P

D = 2048
HEADS = 8
HEAD = 128
STEP = 20
beta_one = 0.9
beta_two = 0.95
learn_rate = 0.001
teacher_keep = 0.996
clip_level = 2.0
tiny_epsilon = 1e-08


def adamw(parameter, first_moment, second_moment, gradient, clip_factor, weight_decay, shadow):
    scaled = gradient * clip_factor
    first_new = beta_one * first_moment + (1.0 - beta_one) * scaled
    second_new = beta_two * second_moment + (1.0 - beta_two) * scaled * scaled
    corr_one = 1.0 - beta_one**STEP
    corr_two = 1.0 - beta_two**STEP
    direction = first_new / corr_one / (jnp.sqrt(second_new / corr_two) + tiny_epsilon)
    parameter_new = parameter - learn_rate * (direction + weight_decay * parameter)
    shadow_new = teacher_keep * shadow + (1.0 - teacher_keep) * parameter_new
    return (parameter_new, first_new, second_new, shadow_new)


def shards(
    grad_part,
    gain_grad_part,
    master,
    moment_one,
    moment_two,
    teacher,
    gain_master,
    gain_moment_one,
    gain_moment_two,
    gain_teacher,
):
    tensor_count = lax.axis_size("tensor")
    local_gain = gain_grad_part[0, 0, 0].astype(jnp.float32)
    local_gain = lax.psum(local_gain, "tensor")
    local_grad = grad_part[0, 0].astype(jnp.float32)
    owned_rows, owned_gain = (
        lax.psum_scatter(local_grad, "fsdp", scatter_dimension=0, tiled=True),
        lax.psum_scatter(local_gain, "fsdp", scatter_dimension=0, tiled=True),
    )
    owned_rows, owned_gain = lax.psum((owned_rows, owned_gain), "dp")
    own_squares = jnp.sum(owned_rows * owned_rows) + jnp.sum(owned_gain * owned_gain) / tensor_count
    total_squares = lax.psum(own_squares, ("fsdp", "tensor"))
    clip_limit = clip_level * math.sqrt(D * HEADS * HEAD + D)
    clip_factor = clip_limit / (jnp.sqrt(total_squares) + 1e-06)
    matrix_state = adamw(master, moment_one, moment_two, owned_rows, clip_factor, 0.1, teacher)
    gain_state = adamw(
        gain_master, gain_moment_one, gain_moment_two, owned_gain, clip_factor, 0.0, gain_teacher
    )
    weights, gain_weights = (
        lax.all_gather(matrix_state[0].astype(jnp.bfloat16), "fsdp", axis=0, tiled=True),
        lax.all_gather(gain_state[0].astype(jnp.bfloat16), "fsdp", axis=0, tiled=True),
    )
    return (
        weights,
        gain_weights,
        matrix_state[0],
        matrix_state[1],
        matrix_state[2],
        matrix_state[3],
        gain_state[0],
        gain_state[1],
        gain_state[2],
        gain_state[3],
    )


def solution(mesh):
    return jax.shard_map(
        shards,
        mesh=mesh,
        in_specs=(
            P("dp", "fsdp", None, "tensor"),
            P("dp", "fsdp", "tensor", None),
            P("fsdp", "tensor"),
            P("fsdp", "tensor"),
            P("fsdp", "tensor"),
            P("fsdp", "tensor"),
            P("fsdp"),
            P("fsdp"),
            P("fsdp"),
            P("fsdp"),
        ),
        out_specs=(
            P(None, "tensor"),
            P(),
            P("fsdp", "tensor"),
            P("fsdp", "tensor"),
            P("fsdp", "tensor"),
            P("fsdp", "tensor"),
            P("fsdp"),
            P("fsdp"),
            P("fsdp"),
            P("fsdp"),
        ),
        check_vma=False,
    )
```

profile of v0, /device:TPU:2, one launch (start us, length us, event | category | flops | bytes accessed | tf_op | source)
XLA Modules:
  0.0 377.3 jit_solution(621989605081140635)
XLA Ops:
  7.2 0.0 copy-start.5
  7.2 0.0 copy-start.2
  7.2 0.0 copy-start.3
  7.2 0.0 copy-start.4
  7.2 0.0 copy-start.1
  7.2 0.0 reduce-scatter.2.cloned.1.call-start
  7.3 2.9 bitcast_convert_fusion
  10.1 0.0 copy-start.6
  10.1 0.0 copy-start.7
  10.1 0.0 copy-start.8
  10.1 0.0 copy-start.9
  10.1 0.0 reduce-scatter.2.cloned.1.call-update
  10.2 0.0 all-reduce.3.cloned.1.call-start
  10.2 78.5 %reduce-scatter.2.cloned.1.call-done = f32[128,256]{1,0:T(8,128)} async-done(((f32[2048,256]{1,0:T(8,128)}), f32[128,256]{1,0:T(8,128)}) %reduce-scatter.2.cloned.1.call-update) | async-done | bytes 131088 | tf_op jit(solution)/shard_map/reduce_scatter | solution.py:48
  88.7 0.0 all-reduce.3.cloned.1.call-update
  88.7 0.0 all-gather.3.cloned.1.call-start
  88.8 0.0 copy-done.5
  88.8 1.3 dynamic-slice
  90.7 28.9 %all-reduce = f32[2048]{0:T(1024)S(1)} all-reduce(f32[2048]{0:T(1024)S(1)} %bitcast.8), channel_id=3, replica_groups=mesh['dp'=8,'fsdp'=16,'tensor'=4] {'fsdp'}, use_global_device_ids=true, to_apply=%region_4.0.clone | all-reduce | flops 2048 | bytes 16384
  119.6 0.1 dynamic-slice.1
  119.7 6.0 %psum.32 = f32[128]{0:T(128)S(1)} all-reduce(f32[128]{0:T(128)S(1)} %dynamic-slice.1), channel_id=1, replica_groups=mesh['dp'=8,'fsdp'=16,'tensor'=4] {'tensor'}, use_global_device_ids=true, to_apply=%region_3.0 | all-reduce | flops 128 | bytes 1024 | tf_op jit(solution)/shard_map/psum | solution.py:45
  125.7 22.9 %psum.30 = f32[128]{0:T(128)S(1)} all-reduce(f32[128]{0:T(128)S(1)} %psum.32), channel_id=1, replica_groups=mesh['dp'=8,'fsdp'=16,'tensor'=4] {'dp'}, use_global_device_ids=true, to_apply=%region_5.0 | all-reduce | flops 128 | bytes 1024 | tf_op jit(solution)/shard_map/psum | solution.py:51
  148.6 0.6 multiply_reduce_fusion.1
  149.8 38.0 %all-reduce.3.cloned.1.call-done = f32[128,256]{1,0:T(8,128)} async-done(((f32[128,256]{1,0:T(8,128)}), f32[128,256]{1,0:T(8,128)}) %all-reduce.3.cloned.1.call-update) | async-done | bytes 131088 | tf_op jit(solution)/shard_map/psum | solution.py:51
  187.8 1.5 multiply_reduce_fusion
  190.0 102.3 %psum.31 = f32[]{:T(128)} all-reduce(f32[]{:T(128)S(6)} %add.54), channel_id=1, replica_groups=mesh['dp'=8,'fsdp'=16,'tensor'=4] {'fsdp','tensor'}, use_global_device_ids=true, to_apply=%region_7.0 | all-reduce | flops 1 | bytes 8 | tf_op jit(solution)/shard_map/psum | solution.py:53
  293.0 0.0 copy-done.2
  293.0 0.0 copy-done.3
  293.0 0.0 copy-done.4
  293.0 0.0 copy-done.1
  293.0 1.7 multiply_add_fusion
  294.7 0.0 copy-start
  294.7 0.7 convert_element_type.22
  295.4 0.0 all-gather.3.cloned.1.call-update
  295.4 0.0 copy-done.6
  295.4 0.0 copy-done.7
  295.5 0.0 copy-done.8
  295.5 0.0 copy-done.9
  295.5 0.5 multiply_add_fusion.2
  296.0 0.0 copy-start.10
  296.0 29.8 %all-gather = bf16[16,1,128]{2,1,0:T(2,128)(2,1)S(1)} all-gather(bf16[1,1,128]{2,1,0:T(2,128)(2,1)S(1)} %convert_bitcast_fusion), channel_id=1, replica_groups=mesh['dp'=8,'fsdp'=16,'tensor'=4] {'fsdp'}, dimensions={0}, use_global_device_ids=true | all-gather | bytes 4352 | tf_op jit(solution)/shard_map/all_gather | solution.py:62
  325.8 0.6 reduce
  326.5 42.0 %all-gather.3.cloned.1.call-done = bf16[2048,256]{1,0:T(8,128)(2,1)} async-done(((bf16[128,256]{1,0:T(8,128)(2,1)}), bf16[2048,256]{1,0:T(8,128)(2,1)}) %all-gather.3.cloned.1.call-update) | async-done | bytes 1048592 | tf_op jit(solution)/shard_map/all_gather | solution.py:61
  368.5 2.3 copy.22
  370.8 0.0 copy-done
  370.8 0.0 copy-done.10
  (2 shorter events, 0.0 us)
Async XLA Ops:
  7.2 81.6 %copy-start.5 = (bf16[1,1,1,2048]{3,2,1,0:T(2,128)(2,1)S(1)}, bf16[1,1,1,2048]{3,2,1,0:T(2,128)(2,1)}, u32[]{:S(2)}) copy-start(bf16[1,1,1,2048]{3,2,1,0:T(2,128)(2,1)} %param.11) | copy-start | bytes 12292
  7.2 285.8 %copy-start.2 = (f32[128,256]{1,0:T(8,128)S(1)}, f32[128,256]{1,0:T(8,128)}, u32[]{:S(2)}) copy-start(f32[128,256]{1,0:T(8,128)} %param.12) | copy-start | bytes 393220
  7.2 285.8 %copy-start.3 = (f32[128,256]{1,0:T(8,128)S(1)}, f32[128,256]{1,0:T(8,128)}, u32[]{:S(2)}) copy-start(f32[128,256]{1,0:T(8,128)} %param.13) | copy-start | bytes 393220
  7.2 285.8 %copy-start.4 = (f32[128,256]{1,0:T(8,128)S(1)}, f32[128,256]{1,0:T(8,128)}, u32[]{:S(2)}) copy-start(f32[128,256]{1,0:T(8,128)} %param.14) | copy-start | bytes 393220
  7.2 285.8 %copy-start.1 = (f32[128,256]{1,0:T(8,128)S(1)}, f32[128,256]{1,0:T(8,128)}, u32[]{:S(2)}) copy-start(f32[128,256]{1,0:T(8,128)} %param.15) | copy-start | bytes 393220
  7.2 81.5 %reduce-scatter.2.cloned.1.call-start = ((), (), s32[]{:S(2)}) async-start(), calls=%async_computation.1 | async-start | bytes 2228224 | tf_op jit(solution)/shard_map/reduce_scatter | solution.py:48
  10.1 285.3 %copy-start.6 = (f32[128]{0:T(128)S(1)}, f32[128]{0:T(128)}, u32[]{:S(2)}) copy-start(f32[128]{0:T(128)} %param.19) | copy-start | bytes 1540
  10.1 285.3 %copy-start.7 = (f32[128]{0:T(128)S(1)}, f32[128]{0:T(128)}, u32[]{:S(2)}) copy-start(f32[128]{0:T(128)} %param.16) | copy-start | bytes 1540
  10.1 285.3 %copy-start.8 = (f32[128]{0:T(128)S(1)}, f32[128]{0:T(128)}, u32[]{:S(2)}) copy-start(f32[128]{0:T(128)} %param.17) | copy-start | bytes 1540
  10.1 285.3 %copy-start.9 = (f32[128]{0:T(128)S(1)}, f32[128]{0:T(128)}, u32[]{:S(2)}) copy-start(f32[128]{0:T(128)} %param.18) | copy-start | bytes 1540
  10.2 177.6 %all-reduce.3.cloned.1.call-start = ((), (), s32[]{:S(2)}) async-start(), calls=%async_computation.2 | async-start | bytes 262144 | tf_op jit(solution)/shard_map/psum | solution.py:51
  88.7 279.8 %all-gather.3.cloned.1.call-start = ((), (), s32[]{:S(2)}) async-start(), calls=%async_computation.3 | async-start | bytes 1114112 | tf_op jit(solution)/shard_map/all_gather | solution.py:61
  294.7 76.1 %copy-start = (f32[128,256]{1,0:T(8,128)}, f32[128,256]{1,0:T(8,128)S(1)}, u32[]{:S(2)}) copy-start(f32[128,256]{1,0:T(8,128)S(1)} %get-tuple-element.30) | copy-start | bytes 393220
  296.0 74.8 %copy-start.10 = (f32[128]{0:T(128)}, f32[128]{0:T(128)S(1)}, u32[]{:S(2)}) copy-start(f32[128]{0:T(128)S(1)} %get-tuple-element.34) | copy-start | bytes 1540
Sparse Core Ops, SparseCore 0:
  10.9 77.7 reduce-scatter.1
  91.6 96.1 all-reduce.2
  295.6 72.9 all-gather.2
where the time goes:
time: 378 us; the launch traced here: 377 us
  blocking collectives  190 us (50%)
  waiting for transfers between devices  159 us (42%)
  between operations  16.6 us (4%)
  other arithmetic  8.58 us (2%)
    psum x1, blocking collectives, shards(): total_squares = lax.psum(own_squares, ('fsdp', 'tensor'))  102 us
    reduce_scatter x1, waiting for transfers between devices, shards(): lax.psum_scatter(local_grad, 'fsdp', scatter_dimension=0, tiled=True)  78.5 us
    all_gather x1, waiting for transfers between devices, shards(): lax.all_gather(matrix_state[0].astype(jnp.bfloat16), 'fsdp', axis=0, tile...  42 us
    psum x1, waiting for transfers between devices, shards(): owned_rows, owned_gain = lax.psum((owned_rows, owned_gain), 'dp')  38 us
    all_gather x1, blocking collectives, shards(): lax.all_gather(gain_state[0].astype(jnp.bfloat16), 'fsdp', axis=0, tiled=...  29.8 us
    unnamed x1, blocking collectives  28.9 us
    psum x1, blocking collectives, shards(): owned_rows, owned_gain = lax.psum((owned_rows, owned_gain), 'dp')  22.9 us
  transfers between devices with their start and end apart: 3, of which 3 were waited for; matrix products, arithmetic and copies ran while one was open for 1% of the time, Pallas kernels for 0%

commit v1 on v0

--- a/solution.py
+++ b/solution.py
@@ -58,7 +58,15 @@
         gain_master, gain_moment_one, gain_moment_two, owned_gain, clip_factor, 0.0, gain_teacher
     )
     weights, gain_weights = (
-        lax.all_gather(matrix_state[0].astype(jnp.bfloat16), "fsdp", axis=0, tiled=True),
+        jnp.concatenate(
+            lax.all_to_all(
+                jnp.stack([matrix_state[0].astype(jnp.bfloat16)] * lax.axis_size("fsdp")),
+                "fsdp",
+                0,
+                0,
+            ),
+            axis=0,
+        ),
         lax.all_gather(gain_state[0].astype(jnp.bfloat16), "fsdp", axis=0, tiled=True),
     )
     return (

time: 378 us -> 390 us (1.032)
  the two profiles are of different devices: /device:TPU:2 before, /device:TPU:32 now
where the time goes in v1:
time: 390 us; the launch traced here: 389 us
  blocking collectives  225 us (58%)
  waiting for transfers between devices  116 us (30%)
  starting transfers between devices  19.6 us (5%)
  between operations  16.9 us (4%)
  other arithmetic  7.93 us (2%)
    psum x1, blocking collectives, shards(): total_squares = lax.psum(own_squares, ('fsdp', 'tensor'))  98.4 us
    reduce_scatter x1, waiting for transfers between devices, shards(): lax.psum_scatter(local_grad, 'fsdp', scatter_dimension=0, tiled=True)  77.6 us
    all_gather x1, blocking collectives, shards(): lax.all_gather(gain_state[0].astype(jnp.bfloat16), 'fsdp', axis=0, tiled=...  68.2 us
    psum x1, waiting for transfers between devices, shards(): owned_rows, owned_gain = lax.psum((owned_rows, owned_gain), 'dp')  38.6 us
    unnamed x1, blocking collectives  28.4 us
    psum x1, blocking collectives, shards(): owned_rows, owned_gain = lax.psum((owned_rows, owned_gain), 'dp')  24.1 us
    all_to_all x1, starting transfers between devices, shards(): lax.all_to_all(jnp.stack([matrix_state[0].astype(jnp.bfloat16)] * lax.axi...  19.5 us
  transfers between devices with their start and end apart: 3, of which 2 were waited for; matrix products, arithmetic and copies ran while one was open for 1% of the time, Pallas kernels for 0%

profile of v1, /device:TPU:32, one launch (start us, length us, event | category | flops | bytes accessed | tf_op | source)
XLA Modules:
  0.0 389.2 jit_solution(686227310949529390)
XLA Ops:
  7.2 0.0 copy-start.5
  7.2 0.0 copy-start.2
  7.2 0.0 copy-start.3
  7.2 0.0 copy-start.4
  7.2 0.0 copy-start.1
  7.2 0.0 reduce-scatter.2.cloned.1.call-start
  7.3 2.9 bitcast_convert_fusion
  10.1 0.0 reduce-scatter.2.cloned.1.call-update
  10.2 0.0 all-reduce.3.cloned.1.call-start
  10.2 77.6 %reduce-scatter.2.cloned.1.call-done = f32[128,256]{1,0:T(8,128)} async-done(((f32[2048,256]{1,0:T(8,128)}), f32[128,256]{1,0:T(8,128)}) %reduce-scatter.2.cloned.1.call-update) | async-done | bytes 131088 | tf_op jit(solution)/shard_map/reduce_scatter | solution.py:48
  87.8 0.0 all-reduce.3.cloned.1.call-update
  87.9 0.0 copy-done.5
  87.9 1.3 dynamic-slice
  89.8 28.4 %all-reduce = f32[2048]{0:T(1024)S(1)} all-reduce(f32[2048]{0:T(1024)S(1)} %bitcast.10), channel_id=3, replica_groups=mesh['dp'=8,'fsdp'=16,'tensor'=4] {'fsdp'}, use_global_device_ids=true, to_apply=%region_4.0.clone | all-reduce | flops 2048 | bytes 16384
  118.3 0.1 dynamic-slice.1
  118.4 6.0 %psum.32 = f32[128]{0:T(128)S(1)} all-reduce(f32[128]{0:T(128)S(1)} %dynamic-slice.1), channel_id=1, replica_groups=mesh['dp'=8,'fsdp'=16,'tensor'=4] {'tensor'}, use_global_device_ids=true, to_apply=%region_3.0 | all-reduce | flops 128 | bytes 1024 | tf_op jit(solution)/shard_map/psum | solution.py:45
  124.4 24.1 %psum.30 = f32[128]{0:T(128)S(1)} all-reduce(f32[128]{0:T(128)S(1)} %psum.32), channel_id=1, replica_groups=mesh['dp'=8,'fsdp'=16,'tensor'=4] {'dp'}, use_global_device_ids=true, to_apply=%region_5.0 | all-reduce | flops 128 | bytes 1024 | tf_op jit(solution)/shard_map/psum | solution.py:51
  148.5 0.6 multiply_reduce_fusion.1
  149.8 38.6 %all-reduce.3.cloned.1.call-done = f32[128,256]{1,0:T(8,128)} async-done(((f32[128,256]{1,0:T(8,128)}), f32[128,256]{1,0:T(8,128)}) %all-reduce.3.cloned.1.call-update) | async-done | bytes 131088 | tf_op jit(solution)/shard_map/psum | solution.py:51
  188.3 1.5 multiply_reduce_fusion
  190.5 98.4 %psum.31 = f32[]{:T(128)} all-reduce(f32[]{:T(128)S(6)} %add.54), channel_id=1, replica_groups=mesh['dp'=8,'fsdp'=16,'tensor'=4] {'fsdp','tensor'}, use_global_device_ids=true, to_apply=%region_7.0 | all-reduce | flops 1 | bytes 8 | tf_op jit(solution)/shard_map/psum | solution.py:53
  289.6 0.0 copy-done.2
  289.6 0.0 copy-done.3
  289.6 0.0 copy-done.4
  289.7 0.0 copy-done.1
  289.7 0.0 copy-start.6
  289.7 0.0 copy-start.7
  289.7 0.0 copy-start.8
  289.7 0.0 copy-start.9
  289.7 1.7 multiply_add_fusion
  291.5 0.0 copy-start
  291.5 1.1 stack.2
  292.5 19.5 %all-to-all-start = ((bf16[16,128,256]{2,1,0:T(8,128)(2,1)}), bf16[16,128,256]{2,1,0:T(8,128)(2,1)S(1)}, u32[]{:S(2)}, u32[]{:S(2)}) async-start(bf16[16,128,256]{2,1,0:T(8,128)(2,1)} %stack.2), calls=%async_computation.1 | async-start | bytes 2097152 | tf_op jit(solution)/shard_map/all_to_all | solution.py:62
  312.0 0.0 copy-done.6
  312.0 0.0 copy-done.7
  312.0 0.0 copy-done.8
  312.1 0.0 copy-done.9
  312.1 0.5 multiply_add_fusion.2
  312.6 0.0 copy-start.10
  312.6 68.2 %all-gather = bf16[16,1,128]{2,1,0:T(2,128)(2,1)S(1)} all-gather(bf16[1,1,128]{2,1,0:T(2,128)(2,1)S(1)} %convert_bitcast_fusion), channel_id=1, replica_groups=mesh['dp'=8,'fsdp'=16,'tensor'=4] {'fsdp'}, dimensions={0}, use_global_device_ids=true | all-gather | bytes 4352 | tf_op jit(solution)/shard_map/all_gather | solution.py:70
  380.8 0.6 reduce
  381.4 0.0 all-to-all-done
  381.4 1.0 copy.22
  382.4 0.0 copy-done
  382.4 0.0 copy-done.10
  (3 shorter events, 0.0 us)
Async XLA Ops:
  7.2 80.7 %copy-start.5 = (bf16[1,1,1,2048]{3,2,1,0:T(2,128)(2,1)S(1)}, bf16[1,1,1,2048]{3,2,1,0:T(2,128)(2,1)}, u32[]{:S(2)}) copy-start(bf16[1,1,1,2048]{3,2,1,0:T(2,128)(2,1)} %param.11) | copy-start | bytes 12292
  7.2 282.4 %copy-start.2 = (f32[128,256]{1,0:T(8,128)S(1)}, f32[128,256]{1,0:T(8,128)}, u32[]{:S(2)}) copy-start(f32[128,256]{1,0:T(8,128)} %param.12) | copy-start | bytes 393220
  7.2 282.4 %copy-start.3 = (f32[128,256]{1,0:T(8,128)S(1)}, f32[128,256]{1,0:T(8,128)}, u32[]{:S(2)}) copy-start(f32[128,256]{1,0:T(8,128)} %param.13) | copy-start | bytes 393220
  7.2 282.4 %copy-start.4 = (f32[128,256]{1,0:T(8,128)S(1)}, f32[128,256]{1,0:T(8,128)}, u32[]{:S(2)}) copy-start(f32[128,256]{1,0:T(8,128)} %param.14) | copy-start | bytes 393220
  7.2 282.4 %copy-start.1 = (f32[128,256]{1,0:T(8,128)S(1)}, f32[128,256]{1,0:T(8,128)}, u32[]{:S(2)}) copy-start(f32[128,256]{1,0:T(8,128)} %param.15) | copy-start | bytes 393220
  7.2 80.6 %reduce-scatter.2.cloned.1.call-start = ((), (), s32[]{:S(2)}) async-start(), calls=%async_computation.2 | async-start | bytes 2228224 | tf_op jit(solution)/shard_map/reduce_scatter | solution.py:48
  10.2 178.2 %all-reduce.3.cloned.1.call-start = ((), (), s32[]{:S(2)}) async-start(), calls=%async_computation.3 | async-start | bytes 262144 | tf_op jit(solution)/shard_map/psum | solution.py:51
  289.7 22.4 %copy-start.6 = (f32[128]{0:T(128)S(1)}, f32[128]{0:T(128)}, u32[]{:S(2)}) copy-start(f32[128]{0:T(128)} %param.19) | copy-start | bytes 1540
  289.7 22.4 %copy-start.7 = (f32[128]{0:T(128)S(1)}, f32[128]{0:T(128)}, u32[]{:S(2)}) copy-start(f32[128]{0:T(128)} %param.16) | copy-start | bytes 1540
  289.7 22.3 %copy-start.8 = (f32[128]{0:T(128)S(1)}, f32[128]{0:T(128)}, u32[]{:S(2)}) copy-start(f32[128]{0:T(128)} %param.17) | copy-start | bytes 1540
  289.7 22.3 %copy-start.9 = (f32[128]{0:T(128)S(1)}, f32[128]{0:T(128)}, u32[]{:S(2)}) copy-start(f32[128]{0:T(128)} %param.18) | copy-start | bytes 1540
  291.5 90.9 %copy-start = (f32[128,256]{1,0:T(8,128)}, f32[128,256]{1,0:T(8,128)S(1)}, u32[]{:S(2)}) copy-start(f32[128,256]{1,0:T(8,128)S(1)} %get-tuple-element.30) | copy-start | bytes 393220
  292.5 88.9 %all-to-all-start = ((bf16[16,128,256]{2,1,0:T(8,128)(2,1)}), bf16[16,128,256]{2,1,0:T(8,128)(2,1)S(1)}, u32[]{:S(2)}, u32[]{:S(2)}) async-start(bf16[16,128,256]{2,1,0:T(8,128)(2,1)} %stack.2), calls=%async_computation.1 | async-start | bytes 2097152 | tf_op jit(solution)/shard_map/all_to_all | solution.py:62
  312.6 69.8 %copy-start.10 = (f32[128]{0:T(128)}, f32[128]{0:T(128)S(1)}, u32[]{:S(2)}) copy-start(f32[128]{0:T(128)S(1)} %get-tuple-element.34) | copy-start | bytes 1540
Sparse Core Ops, SparseCore 0:
  10.9 76.9 reduce-scatter.1
  90.7 97.5 all-reduce.2
